TPU v7x, 512 devices: a whole 4x4x16 slice. The times are simulated.
512 devices in a mesh: seq: 128 (over x, z, core), rep: 4 (over y).
Axes of the slice: x: 4, y: 4, z: 16, core: 2. Of those that a mesh axis runs over, the one named last changes fastest.
Arguments:
- tokens: bfloat16 [16384, 1440], P('seq'), may hold values from -36 to 36
- norm_gain: float32 [1440], replicated, may hold values from 0.1 to 1.9
- expert_ids: int32 [16384, 4], P('seq'), may hold values from 0 to 127, all different within a row; in each aligned block of 128 rows (0 to 127, 128 to 255, ...) at most 8 rows name the same one
- route_weights: float32 [16384, 4], P('seq'), may hold values from 0.1 to 0.6
- gate_weight: bfloat16 [128, 1440, 1440], P('seq', None, 'rep'), may hold values from -0.15625 to 0.15625
- gate_bias: float32 [128, 1440], P('seq', 'rep'), may hold values from -3 to 3
- up_weight: bfloat16 [128, 1440, 1440], P('seq', None, 'rep'), may hold values from -0.15625 to 0.15625
- up_bias: float32 [128, 1440], P('seq', 'rep'), may hold values from -3 to 3
- down_weight: bfloat16 [128, 1440, 1440], P('seq', 'rep'), may hold values from -0.15625 to 0.15625
- down_bias: float32 [128, 1440], P('seq', 'rep'), may hold values from -3 to 3
Outputs:
- mixed: bfloat16 [16384, 1440], P('seq', 'rep')
Inputs may be any that keep to these rules, and one draw needn't show every extreme that they name: `expert_ids`: each row names 4 different experts. Among the 128 rows of one index of seq no expert is named more than 8 times, and in every draw some expert is named exactly 8 times by the rows of one index.
All inputs are finite; a program needn't handle non-finite values.
Results may differ from a plain program's by a relative error of at most 0.014.
Values may be sent and summed in bfloat16 or wider, within the bound.
A program may use at most 64 MiB of HBM per device.

v0:
```python
import jax
import jax.numpy as jnp
from jax import lax
from jax.sharding import PartitionSpec as P


def on_device(
    tokens,
    norm_gain,
    expert_ids,
    route_weights,
    gate_weight,
    gate_bias,
    up_weight,
    up_bias,
    down_weight,
    down_bias,
):
    tok_rows, features = tokens.shape
    per_token = expert_ids.shape[1]
    experts = lax.axis_size("seq")
    groups = lax.axis_size("rep")
    quarter = features // groups
    capacity = 2 * tok_rows * per_token // experts
    values = tokens.astype(jnp.float32)
    normed = (
        values * lax.rsqrt(jnp.mean(values * values, axis=-1, keepdims=True) + 1e-05) * norm_gain
    ).astype(jnp.bfloat16)
    flat_ids = expert_ids.reshape(-1)
    onehot = (flat_ids[:, None] == jnp.arange(experts, dtype=jnp.int32)[None, :]).astype(jnp.int32)
    before = jnp.cumsum(onehot, axis=0) - onehot
    slot_index = jnp.sum(before * onehot, axis=1)
    destination = flat_ids * capacity + slot_index
    owner_row = jnp.arange(tok_rows * per_token, dtype=jnp.int32) // per_token
    buffer = jnp.zeros((experts * capacity, normed.shape[1]), jnp.bfloat16)
    buffer = buffer.at[destination].set(normed[owner_row])
    received = lax.all_to_all(
        buffer.reshape(experts, capacity, normed.shape[1]),
        "seq",
        split_axis=0,
        concat_axis=0,
        tiled=True,
    )
    in_rows = received.reshape(-1, features)
    gate_pre = jnp.dot(in_rows, gate_weight[0], preferred_element_type=jnp.float32) + gate_bias[0]
    up_pre = jnp.dot(in_rows, up_weight[0], preferred_element_type=jnp.float32) + up_bias[0]
    activated = (gate_pre * jax.nn.sigmoid(1.702 * gate_pre) * (up_pre + 1.0)).astype(jnp.bfloat16)
    partial_value = jnp.dot(activated, down_weight[0], preferred_element_type=jnp.float32)
    rounded = lax.optimization_barrier(partial_value.astype(jnp.bfloat16))
    partial_value = rounded.reshape(received.shape[0], received.shape[1], features)
    summed = lax.psum_scatter(
        partial_value.astype(jnp.float32).astype(jnp.bfloat16),
        "rep",
        scatter_dimension=2,
        tiled=True,
    ).astype(jnp.float32)
    expert_out = (summed + down_bias[0][None, None, :]).astype(jnp.bfloat16)
    returned = lax.all_to_all(expert_out, "seq", split_axis=0, concat_axis=0, tiled=True)
    picked = returned.reshape(-1, quarter)[destination].reshape(tok_rows, per_token, quarter)
    mixed = jnp.sum(route_weights[:, :, None] * picked.astype(jnp.float32), axis=1)
    return mixed.astype(jnp.bfloat16)


def solution(mesh):
    placed = (
        P("seq", None),
        P(),
        P("seq", None),
        P("seq", None),
        P("seq", None, "rep"),
        P("seq", "rep"),
        P("seq", None, "rep"),
        P("seq", "rep"),
        P("seq", "rep", None),
        P("seq", "rep"),
    )
    return jax.shard_map(
        on_device, mesh=mesh, in_specs=placed, out_specs=P("seq", "rep"), check_vma=False
    )
```

profile of v0, /device:TPU:1, one launch (start us, length us, event | category | flops | bytes accessed | tf_op | source)
XLA Modules:
  0.0 318.3 jit_solution(6020006446976306172)
XLA Ops:
  6.5 0.9 copy.58
  7.7 0.7 broadcast_multiply_fusion
  8.5 0.2 fusion.25
  9.0 0.2 copy.62
  9.2 0.2 fusion.16
  9.4 0.2 fusion.24
  9.7 0.2 fusion.18
  9.8 10.2 %scatter_custom_fusion = bf16[1024,1440]{1,0:T(8,128)(2,1)} fusion(s32[512]{0:T(512)S(1)} %bitcast.46, bf16[128,1440]{1,0:T(8,128)(2,1)S(1)} %fusion.18, s32[1024]{0:T(1024)S(1)} %pad_clamp_fusion.1, bf16[]{:T(256)} %constant.15.clone.1), kind=kCustom, calls=%fused_computation.8 | custom fusion | bytes 2949122 | tf_op jit(solution)/shard_map/scatter | solution.py:36
  20.1 20.9 %all-to-all-start = ((bf16[128,8,1440]{2,1,0:T(8,128)(2,1)}), bf16[128,8,1440]{2,1,0:T(8,128)(2,1)}, u32[]{:S(2)}, u32[]{:S(2)}) async-start(bf16[128,8,1440]{2,1,0:T(8,128)(2,1)} %bitcast.40), calls=%async_computation | async-start | bytes 6291456 | tf_op jit(solution)/shard_map/all_to_all | solution.py:37
  41.1 142.4 %all-to-all-done = bf16[128,8,1440]{2,1,0:T(8,128)(2,1)} async-done(((bf16[128,8,1440]{2,1,0:T(8,128)(2,1)}), bf16[128,8,1440]{2,1,0:T(8,128)(2,1)}, u32[]{:S(2)}, u32[]{:S(2)}) %all-to-all-start) | async-done | bytes 2949152 | tf_op jit(solution)/shard_map/all_to_all | solution.py:37
  183.5 4.4 %fusion = f32[1024,360]{0,1:T(8,128)} fusion(bf16[128,8,1440]{2,1,0:T(8,128)(2,1)} %all-to-all-done, bf16[1,1440,360]{2,1,0:T(8,128)(2,1)S(1)} %copy-done.7), kind=kOutput, calls=%fused_computation.4 | convolution fusion | flops 1061683200 | bytes 5460480 | tf_op jit(solution)/shard_map/dot_general | solution.py:46
  187.9 7.5 %convolution_convert_fusion = bf16[1024,1440]{0,1:T(8,128)(2,1)} fusion(bf16[1,360,1440]{2,1,0:T(8,128)(2,1)S(1)} %copy-done, f32[1024,360]{0,1:T(8,128)} %fusion, bf16[128,8,1440]{2,1,0:T(8,128)(2,1)} %all-to-all-done, bf16[1,1440,360]{2,1,0:T(8,128)(2,1)} %param.14, f32[360]{0:T(512)S(1)} %reduce.1, f32[360]{0:T(512)S(1)} %reduce), kind=kOutput, calls=%fused_computation.3 | convolution fusion | flops 2128527360 | bytes 9449280 | tf_op jit(solution)/shard_map/dot_general | solution.py:48
  195.4 4.6 %copy.63 = bf16[1024,1440]{1,0:T(8,128)(2,1)} copy(bf16[1024,1440]{0,1:T(8,128)(2,1)} %convolution_convert_fusion) | data formatting | bytes 5898240 | tf_op jit(solution)/shard_map/optimization_barrier | solution.py:49
  200.0 5.3 %copy.64 = bf16[128,8,1440]{0,1,2:T(8,128)(2,1)} copy(bf16[128,8,1440]{2,1,0:T(8,128)(2,1)} %bitcast.41) | data formatting | bytes 5898240 | tf_op jit(solution)/shard_map/reshape | solution.py:50
  205.4 0.7 copy-done.6
  206.0 38.7 %reduce-scatter.2.cloned.1.call-done = bf16[128,8,360]{0,1,2:T(8,128)(2,1)} async-done(((bf16[128,8,1440]{0,1,2:T(8,128)(2,1)}), bf16[128,8,360]{0,1,2:T(8,128)(2,1)}) %reduce-scatter.2.cloned.1.call-update) | async-done | bytes 737296 | tf_op jit(solution)/shard_map/reduce_scatter | solution.py:51
  244.7 1.6 add_convert_fusion
  246.3 1.5 copy.65
  247.8 16.7 %all-to-all-start.1 = ((bf16[128,8,360]{2,1,0:T(8,128)(2,1)}), bf16[128,8,360]{2,1,0:T(8,128)(2,1)S(1)}, u32[]{:S(2)}, u32[]{:S(2)}) async-start(bf16[128,8,360]{2,1,0:T(8,128)(2,1)} %copy.65), calls=%async_computation.2 | async-start | bytes 1572864 | tf_op jit(solution)/shard_map/all_to_all | solution.py:58
  264.6 43.3 %all-to-all-done.1 = bf16[128,8,360]{2,1,0:T(8,128)(2,1)S(1)} async-done(((bf16[128,8,360]{2,1,0:T(8,128)(2,1)}), bf16[128,8,360]{2,1,0:T(8,128)(2,1)S(1)}, u32[]{:S(2)}, u32[]{:S(2)}) %all-to-all-start.1) | async-done | bytes 737312 | tf_op jit(solution)/shard_map/all_to_all | solution.py:58
  308.0 1.9 gather_fusion
  309.9 0.2 reshape.120
  310.1 0.6 multiply_reduce_fusion
  310.7 0.8 copy.66
  (37 shorter events, 0.9 us)
Async XLA Ops:
  6.5 181.4 %copy-start = (bf16[1,360,1440]{2,1,0:T(8,128)(2,1)S(1)}, bf16[1,360,1440]{2,1,0:T(8,128)(2,1)}, u32[]{:S(2)}) copy-start(bf16[1,360,1440]{2,1,0:T(8,128)(2,1)} %param.18) | copy-start | bytes 3110404
  6.5 2.5 copy-start.1
  8.5 1.2 copy-start.2
  20.1 21.0 %copy-start.4 = (f32[1,360]{1,0:T(1,128)S(1)}, f32[1,360]{1,0:T(1,128)}, u32[]{:S(2)}) copy-start(f32[1,360]{1,0:T(1,128)} %param.15) | copy-start | bytes 4324
  20.1 21.0 %copy-start.5 = (f32[1,360]{1,0:T(1,128)S(1)}, f32[1,360]{1,0:T(1,128)}, u32[]{:S(2)}) copy-start(f32[1,360]{1,0:T(1,128)} %param.17) | copy-start | bytes 4324
  20.1 163.4 %copy-start.7 = (bf16[1,1440,360]{2,1,0:T(8,128)(2,1)S(1)}, bf16[1,1440,360]{2,1,0:T(8,128)(2,1)}, u32[]{:S(2)}) copy-start(bf16[1,1440,360]{2,1,0:T(8,128)(2,1)} %param.16) | copy-start | bytes 3110404
  20.1 163.4 %all-to-all-start = ((bf16[128,8,1440]{2,1,0:T(8,128)(2,1)}), bf16[128,8,1440]{2,1,0:T(8,128)(2,1)}, u32[]{:S(2)}, u32[]{:S(2)}) async-start(bf16[128,8,1440]{2,1,0:T(8,128)(2,1)} %bitcast.40), calls=%async_computation | async-start | bytes 6291456 | tf_op jit(solution)/shard_map/all_to_all | solution.py:37
  41.0 203.7 %reduce-scatter.2.cloned.1.call-start = ((), (), s32[]{:S(2)}) async-start(), calls=%async_computation.3 | async-start | bytes 3686400 | tf_op jit(solution)/shard_map/reduce_scatter | solution.py:51
  205.3 0.7 copy-start.6
  246.3 18.2 %copy-start.3 = (f32[128,4]{0,1:T(4,128)S(1)}, f32[128,4]{0,1:T(4,128)}, u32[]{:S(2)}) copy-start(f32[128,4]{0,1:T(4,128)} %param.13) | copy-start | bytes 6148
  247.8 60.1 %all-to-all-start.1 = ((bf16[128,8,360]{2,1,0:T(8,128)(2,1)}), bf16[128,8,360]{2,1,0:T(8,128)(2,1)S(1)}, u32[]{:S(2)}, u32[]{:S(2)}) async-start(bf16[128,8,360]{2,1,0:T(8,128)(2,1)} %copy.65), calls=%async_computation.2 | async-start | bytes 1572864 | tf_op jit(solution)/shard_map/all_to_all | solution.py:58
Sparse Core Ops, SparseCore 0:
  205.5 39.1 reduce-scatter.1
where the time goes:
time: 319 us; the launch traced here: 318 us
  waiting for transfers between devices  224 us (70%)
  starting transfers between devices  37.6 us (12%)
  local copies, waits for them, and re-layouts  27.1 us (8%)
  between operations  13.6 us (4%)
  matrix products  11.9 us (4%)
  other arithmetic  3.72 us (1%)
    all_to_all x1, waiting for transfers between devices, on_device(): lax.all_to_all(buffer.reshape(experts, capacity, normed.shape[1]), 'seq',...  142 us
    all_to_all x1, waiting for transfers between devices, on_device(): lax.all_to_all(expert_out, 'seq', split_axis=0, concat_axis=0, tiled=True)  43.3 us
    reduce_scatter x1, waiting for transfers between devices, on_device(): lax.psum_scatter(partial_value.astype(jnp.float32).astype(jnp.bfloat16),...  38.7 us
    all_to_all x1, starting transfers between devices, on_device(): lax.all_to_all(buffer.reshape(experts, capacity, normed.shape[1]), 'seq',...  20.9 us
    all_to_all x1, starting transfers between devices, on_device(): lax.all_to_all(expert_out, 'seq', split_axis=0, concat_axis=0, tiled=True)  16.7 us
    scatter x1, local copies, waits for them, and re-layouts, on_device(): buffer = buffer.at[destination].set(normed[owner_row])  10.2 us
    dot_general x1, matrix products, on_device(): jnp.dot(activated, down_weight[0], preferred_element_type=jnp.float32)  7.54 us
  transfers between devices with their start and end apart: 3, of which 3 were waited for; matrix products, arithmetic and copies ran while one was open for 0% of the time, Pallas kernels for 0%

commit v1 on v0

v1 whole, which is shorter than its diff:
```python
import functools

import jax
import jax.numpy as jnp
from jax import lax
from jax.experimental import pallas as pl
from jax.experimental.pallas import tpu as pltpu
from jax.sharding import PartitionSpec as P

MESH = pl.DeviceIdType.MESH
BF16, F32 = jnp.bfloat16, jnp.float32

CORES = 2
Z_RING = 16
BLOCK = 384
SLOTS = 8
PAIR = 2 * SLOTS


def kernel(
    x_size,
    z_size,
    own_ref,
    meta_ref,
    bias_ref,
    wg_hbm,
    wu_hbm,
    wd_hbm,
    out_ref,
    tok,
    meta,
    rows_out,
    in_rows,
    w_in,
    w_out,
    wg_s,
    wu_s,
    wd_s,
    part,
    rs_r,
    rs_a,
    rs_b,
    rs_t,
    out_rows,
    back,
    mix,
    acc_s,
    acc_r,
    upper,
    w_sem,
    z_send,
    z_recv,
    m_send,
    m_recv,
    x_send,
    x_recv,
    x_loc,
    y_send,
    y_recv,
    r_send,
    r_recv,
    b_send,
    b_recv,
    b_loc,
    c_send,
    c_recv,
):
    seq, y = lax.axis_index("seq"), lax.axis_index("rep")
    half_z = z_size // 2
    stages = half_z
    group = x_size * CORES
    rows = group * PAIR
    tokens = own_ref.shape[0]
    half = tokens // 2
    quarter = out_ref.shape[1]
    xi = seq // (z_size * CORES)
    zi = (seq // CORES) % z_size
    ci = seq % CORES
    me = xi * CORES + ci

    def at_z(step):
        return (xi * z_size + (zi + z_size + step) % z_size) * CORES + ci

    def at_x(index):
        return ((index // CORES) * z_size + zi) * CORES + index % CORES

    def at_y(step):
        return (y + 4 + step) % 4

    z_up, z_down = at_z(1), at_z(-1)

    barrier = pltpu.get_barrier_semaphore()
    for peer in (z_up, z_down):
        pl.semaphore_signal(barrier, inc=1, device_id=(peer, y), device_id_type=MESH)
    for j in range(1, group):
        pl.semaphore_signal(
            barrier, inc=1, device_id=(at_x((me + j) % group), y), device_id_type=MESH
        )
    for step in (1, -1):
        pl.semaphore_signal(barrier, inc=1, device_id=(seq, at_y(step)), device_id_type=MESH)

    weights = [
        pltpu.make_async_copy(wg_hbm.at[0], wg_s, w_sem.at[0]),
        pltpu.make_async_copy(wu_hbm.at[0], wu_s, w_sem.at[1]),
        pltpu.make_async_copy(wd_hbm.at[0], wd_s, w_sem.at[2]),
    ]
    for copy in weights:
        copy.start()
    pl.semaphore_wait(barrier, 2 + (group - 1) + 2)

    def z_copy(way, k, h, src):
        return pltpu.make_async_remote_copy(
            src_ref=src.at[pl.ds(h * half, half)],
            dst_ref=tok.at[k, way, pl.ds(h * half, half)],
            send_sem=z_send.at[way, k, h],
            recv_sem=z_recv.at[way, k, h],
            device_id=(z_up if way else z_down, y),
            device_id_type=MESH,
        )

    def m_copy(way, k, src):
        return pltpu.make_async_remote_copy(
            src_ref=src,
            dst_ref=meta.at[k, way],
            send_sem=m_send.at[way, k],
            recv_sem=m_recv.at[way, k],
            device_id=(z_up if way else z_down, y),
            device_id_type=MESH,
        )

    for way in (0, 1):
        m_copy(way, way, meta_ref).start()
        for h in (0, 1):
            z_copy(way, way, h, own_ref).start()

    tok[0, 1] = own_ref[...]
    meta[0, 1] = meta_ref[...]
    upper[...] = (
        lax.broadcasted_iota(jnp.int32, (tokens, tokens), 0)
        < lax.broadcasted_iota(jnp.int32, (tokens, tokens), 1)
    ).astype(BF16)

    features, hidden = wg_s.shape
    w_in[...] = jnp.zeros_like(w_in)
    w_out[...] = jnp.zeros_like(w_out)
    for copy in weights:
        copy.wait()
    strip = 144

    @pl.loop(0, features // strip)
    def _(i):
        at = pl.ds(pl.multiple_of(i * strip, 16), strip)
        w_in[at, 0:hidden] = wg_s[at, :]
        w_in[at, BLOCK : BLOCK + hidden] = wu_s[at, :]

    for p in range(4):
        w_out[0:hidden, p * BLOCK : p * BLOCK + quarter] = wd_s[:, p * quarter : (p + 1) * quarter]

    expert = lax.broadcasted_iota(jnp.int32, (group, tokens), 0)
    expert = ((expert // CORES) * z_size + zi) * CORES + expert % CORES
    expert = expert.astype(F32)
    slot = lax.broadcasted_iota(jnp.int32, (group, SLOTS, tokens), 1).astype(F32)

    def x_copy(k, j):
        e = (me + j) % group
        return pltpu.make_async_remote_copy(
            src_ref=rows_out.at[k, e],
            dst_ref=in_rows.at[k, y, me],
            send_sem=x_send.at[k],
            recv_sem=x_recv.at[k],
            device_id=(at_x(e), y),
            device_id_type=MESH,
        )

    def x_local(k):
        return pltpu.make_async_copy(rows_out.at[k, me], in_rows.at[k, y, me], x_loc.at[k])

    def b_copy(k, j):
        e = (me + j) % group
        return pltpu.make_async_remote_copy(
            src_ref=out_rows.at[k, e],
            dst_ref=back.at[k, me],
            send_sem=b_send.at[k],
            recv_sem=b_recv.at[k],
            device_id=(at_x(e), y),
            device_id_type=MESH,
        )

    def b_local(k):
        return pltpu.make_async_copy(out_rows.at[k, me], back.at[k, me], b_loc.at[k])

    def sign(k):
        return 1 - 2 * (k % 2)

    def y_copy(k, kind):
        s = sign(k)
        block = at_y(-s) if kind == 2 else y
        to = at_y(-s) if kind == 1 else at_y(s)
        return pltpu.make_async_remote_copy(
            src_ref=in_rows.at[k, block],
            dst_ref=in_rows.at[k, block],
            send_sem=y_send.at[kind, k],
            recv_sem=y_recv.at[kind, k],
            device_id=(seq, to),
            device_id_type=MESH,
        )

    def r_copy(k, kind):
        s = sign(k)
        to = at_y(-s) if kind == 1 else at_y(s)
        src = rs_t.at[k] if kind == 2 else part.at[k, at_y(2) if kind == 0 else at_y(-s)]
        return pltpu.make_async_remote_copy(
            src_ref=src,
            dst_ref=(rs_r, rs_b, rs_a)[kind].at[k],
            send_sem=r_send.at[kind, k],
            recv_sem=r_recv.at[kind, k],
            device_id=(seq, to),
            device_id_type=MESH,
        )

    def c_copy(way, k, h, to_slot):
        return pltpu.make_async_remote_copy(
            src_ref=acc_s.at[way, k, pl.ds(h * half, half)],
            dst_ref=acc_r.at[way, to_slot, pl.ds(h * half, half)],
            send_sem=c_send.at[way, k, h],
            recv_sem=c_recv.at[way, to_slot, h],
            device_id=(z_down if way else z_up, y),
            device_id_type=MESH,
        )

    def z_stage(k):
        @pl.when(k >= 1)
        def _():
            m_copy(1, k, meta.at[k, 1]).wait_recv()

            @pl.when(k < stages - 1)
            def _():
                m_copy(1, k + 1, meta.at[k, 1]).start()

            for h in (0, 1):
                z_copy(1, k, h, tok.at[k, 1]).wait_recv()

                @pl.when(k < stages - 1)
                def _():
                    z_copy(1, k + 1, h, tok.at[k, 1]).start()

        m_copy(0, k, meta.at[k, 0]).wait_recv()

        @pl.when(k < stages - 1)
        def _():
            m_copy(0, k + 1, meta.at[k, 0]).start()

        for h in (0, 1):
            z_copy(0, k, h, tok.at[k, 0]).wait_recv()

            @pl.when(k < stages - 1)
            def _():
                z_copy(0, k + 1, h, tok.at[k, 0]).start()

    def dispatch(k):
        picks, mixes = [], []
        for j in (0, 1):
            m = meta[k, j]
            hit = jnp.zeros((group, tokens), F32)
            weight = jnp.zeros((group, tokens), F32)
            for c in range(4):
                equal = m[c : c + 1, :] == expert
                hit = jnp.where(equal, 1.0, hit)
                weight = jnp.where(equal, m[4 + c : 5 + c, :], weight)
            rank = jnp.dot(hit.astype(BF16), upper[...], preferred_element_type=F32)
            rank = jnp.where(hit > 0.5, rank, -1.0)
            chosen = rank[:, None, :] == slot
            picks.append(jnp.where(chosen, 1.0, 0.0))
            mixes.append(jnp.where(chosen, weight[:, None, :], 0.0))
        empty = jnp.zeros((group, SLOTS, tokens), F32)

        def both(a, b):
            top = jnp.concatenate([a, empty], axis=2)
            low = jnp.concatenate([empty, b], axis=2)
            return jnp.concatenate([top, low], axis=1).reshape(rows, 2 * tokens)

        pick = both(*picks).astype(BF16)
        got = jnp.dot(pick, tok[k].reshape(2 * tokens, BLOCK), preferred_element_type=F32)
        rows_out[k] = got.astype(BF16).reshape(group, PAIR, BLOCK)
        x_local(k).start()
        for j in range(1, group):
            x_copy(k, j).start()
        blend = both(*mixes).T
        high = blend.astype(BF16)
        mix[k, :, 0:rows] = high
        mix[k, :, rows : 2 * rows] = (blend - high.astype(F32)).astype(BF16)

    def y_start(k):
        x_local(k).wait()
        whole = in_rows.at[k, y, pl.ds(0, group - 1)]
        pltpu.make_async_copy(whole, whole, x_recv.at[k]).wait()
        y_copy(k, 0).start()
        y_copy(k, 1).start()

    def y_relay(k):
        y_copy(k, 0).wait_recv()
        y_copy(k, 2).start()

    def compute(k):
        y_copy(k, 1).wait_recv()
        y_copy(k, 2).wait_recv()
        x = jnp.concatenate([in_rows[k, q].reshape(rows, BLOCK) for q in range(4)], axis=1)
        pre = jnp.dot(x, w_in[...], preferred_element_type=F32)
        gate = pre[:, :BLOCK] + bias_ref[0:1, :]
        up = pre[:, BLOCK:] + bias_ref[1:2, :]
        act = (gate * jax.nn.sigmoid(1.702 * gate) * (up + 1.0)).astype(BF16)
        result = jnp.dot(act, w_out[...], preferred_element_type=F32).astype(BF16)
        for p in range(4):
            part[k, p] = result[:, p * BLOCK : (p + 1) * BLOCK]

    @pl.loop(0, stages + 3)
    def _(t):
        @pl.when(t < stages)
        def _():
            z_stage(t)
            dispatch(t)

        @pl.when((t >= 1) & (t < stages + 1))
        def _():
            y_start(t - 1)

        @pl.when((t >= 2) & (t < stages + 2))
        def _():
            y_relay(t - 2)

        @pl.when(t >= 3)
        def _():
            compute(t - 3)

    def r_start(k):
        r_copy(k, 0).start()
        r_copy(k, 1).start()

    def r_relay(k):
        r_copy(k, 0).wait_recv()
        total = rs_r[k].astype(F32) + part[k, at_y(sign(k))].astype(F32)
        rs_t[k] = total.astype(BF16)
        r_copy(k, 2).start()

    def finish(k):
        r_copy(k, 1).wait_recv()
        r_copy(k, 2).wait_recv()
        total = part[k, y].astype(F32) + rs_b[k].astype(F32) + rs_a[k].astype(F32)
        total = total + bias_ref[2:3, :]
        out_rows[k] = total.astype(BF16).reshape(group, PAIR, BLOCK)
        b_local(k).start()
        for j in range(1, group):
            b_copy(k, j).start()

    def combine(k):
        b_local(k).wait()
        whole = back.at[k, pl.ds(0, group - 1)]
        pltpu.make_async_copy(whole, whole, b_recv.at[k]).wait()
        came = back[k].reshape(rows, BLOCK)
        came = jnp.concatenate([came, came], axis=0)
        both = jnp.dot(mix[k], came, preferred_element_type=F32)
        for h in (0, 1):
            at = pl.ds(h * half, half)
            for way in (0, 1):
                value = both[way * tokens + h * half : way * tokens + (h + 1) * half]

                @pl.when(k == stages - 1)
                def _():
                    acc_s[way, k, at] = value.astype(BF16)

                @pl.when(k < stages - 1)
                def _():
                    c_copy(way, k, h, k).wait_recv()
                    total = value + acc_r[way, k, at].astype(F32)
                    acc_s[way, k, at] = total.astype(BF16)

                if way == 0:
                    c_copy(0, k, h, (k + stages - 1) % stages).start()
                else:

                    @pl.when(k >= 1)
                    def _():
                        c_copy(1, k, h, k - 1).start()

        @pl.when(k == 0)
        def _():
            for h in (0, 1):
                at = pl.ds(h * half, half)
                value = both[tokens + h * half : tokens + (h + 1) * half]
                c_copy(0, 0, h, stages - 1).wait_recv()
                total = value + acc_r[1, 0, at].astype(F32) + acc_r[0, stages - 1, at].astype(F32)
                out_ref[at, :] = total[:, :quarter].astype(out_ref.dtype)

    @pl.loop(0, stages + 3)
    def _(t):
        @pl.when(t < stages)
        def _():
            r_start(stages - 1 - t)

        @pl.when((t >= 1) & (t < stages + 1))
        def _():
            r_relay(stages - t)

        @pl.when((t >= 2) & (t < stages + 2))
        def _():
            finish(stages + 1 - t)

        @pl.when(t >= 3)
        def _():
            combine(stages + 2 - t)

    @pl.loop(0, stages)
    def _(k):
        for way in (0, 1):

            @pl.when(k >= way)
            def _():
                m_copy(way, k, meta_ref).wait_send()
                for h in (0, 1):
                    z_copy(way, k, h, own_ref).wait_send()
                    c_copy(way, k, h, k).wait_send()

        for kind in range(3):
            y_copy(k, kind).wait_send()
            r_copy(k, kind).wait_send()
        sent = rows_out.at[k, pl.ds(0, group - 1)]
        pltpu.make_async_copy(sent, sent, x_send.at[k]).wait()
        sent = out_rows.at[k, pl.ds(0, group - 1)]
        pltpu.make_async_copy(sent, sent, b_send.at[k]).wait()


def on_device(
    tokens,
    norm_gain,
    expert_ids,
    route_weights,
    gate_weight,
    gate_bias,
    up_weight,
    up_bias,
    down_weight,
    down_bias,
):
    tok_rows, features = tokens.shape
    z_size = Z_RING
    x_size = lax.axis_size("seq") // (z_size * CORES)
    hidden = gate_weight.shape[2]
    quarter = features // 4
    stages = z_size // 2
    group = x_size * CORES
    rows = group * PAIR
    values = tokens.astype(F32)
    normed = (
        values * lax.rsqrt(jnp.mean(values * values, axis=-1, keepdims=True) + 1e-05) * norm_gain
    ).astype(BF16)
    normed = jnp.pad(normed, ((0, 0), (0, 4 * BLOCK - features)))
    own = lax.dynamic_slice(normed, (0, lax.axis_index("rep") * BLOCK), (tok_rows, BLOCK))
    meta = jnp.concatenate([expert_ids.T.astype(F32), route_weights.T], axis=0)
    bias = jnp.concatenate([gate_bias, up_bias, down_bias], axis=0)
    bias = jnp.pad(bias, ((0, 5), (0, BLOCK - hidden)))

    block = (stages, rows, BLOCK)
    vmem = pl.BlockSpec(memory_space=pltpu.VMEM)
    hbm = pl.BlockSpec(memory_space=pl.ANY)
    dma = pltpu.SemaphoreType.DMA
    return pl.pallas_call(
        functools.partial(kernel, x_size, z_size),
        out_shape=jax.ShapeDtypeStruct((tok_rows, quarter), BF16),
        in_specs=[vmem, vmem, vmem, hbm, hbm, hbm],
        out_specs=vmem,
        scratch_shapes=[
            pltpu.VMEM((stages, 2, tok_rows, BLOCK), BF16),
            pltpu.VMEM((stages, 2, 8, tok_rows), F32),
            pltpu.VMEM((stages, group, PAIR, BLOCK), BF16),
            pltpu.VMEM((stages, 4, group, PAIR, BLOCK), BF16),
            pltpu.VMEM((4 * BLOCK, 2 * BLOCK), BF16),
            pltpu.VMEM((BLOCK, 4 * BLOCK), BF16),
            pltpu.VMEM(gate_weight.shape[1:], BF16),
            pltpu.VMEM(up_weight.shape[1:], BF16),
            pltpu.VMEM(down_weight.shape[1:], BF16),
            pltpu.VMEM((stages, 4, rows, BLOCK), BF16),
            pltpu.VMEM(block, BF16),
            pltpu.VMEM(block, BF16),
            pltpu.VMEM(block, BF16),
            pltpu.VMEM(block, BF16),
            pltpu.VMEM((stages, group, PAIR, BLOCK), BF16),
            pltpu.VMEM((stages, group, PAIR, BLOCK), BF16),
            pltpu.VMEM((stages, 2 * tok_rows, 2 * rows), BF16),
            pltpu.VMEM((2, stages, tok_rows, BLOCK), BF16),
            pltpu.VMEM((2, stages, tok_rows, BLOCK), BF16),
            pltpu.VMEM((tok_rows, tok_rows), BF16),
            dma((3,)),
            dma((2, stages, 2)),
            dma((2, stages, 2)),
            dma((2, stages)),
            dma((2, stages)),
            dma((stages,)),
            dma((stages,)),
            dma((stages,)),
            dma((3, stages)),
            dma((3, stages)),
            dma((3, stages)),
            dma((3, stages)),
            dma((stages,)),
            dma((stages,)),
            dma((stages,)),
            dma((2, stages, 2)),
            dma((2, stages, 2)),
        ],
        compiler_params=pltpu.CompilerParams(
            collective_id=0, has_side_effects=True, vmem_limit_bytes=56 * 1024 * 1024
        ),
    )(own, meta, bias, gate_weight, up_weight, down_weight)


def solution(mesh):
    placed = (
        P("seq", None),
        P(),
        P("seq", None),
        P("seq", None),
        P("seq", None, "rep"),
        P("seq", "rep"),
        P("seq", None, "rep"),
        P("seq", "rep"),
        P("seq", "rep", None),
        P("seq", "rep"),
    )
    return jax.shard_map(
        on_device, mesh=mesh, in_specs=placed, out_specs=P("seq", "rep"), check_vma=False
    )
```

time: 319 us -> 113 us (0.35)
  waiting for transfers between devices: 224 us -> 0 us
  Pallas kernels: 0 us -> 108 us
  starting transfers between devices: 37.6 us -> 0 us
  local copies, waits for them, and re-layouts: 27.1 us -> 3.53 us
  between operations: 13.6 us -> 0.06 us
  matrix products: 11.9 us -> 0 us
    all_to_all x2 -> x0, waiting for transfers between devices: 186 us -> none  [the longest x1 142 us: on_device(): lax.all_to_all(buffer.reshape(experts, capacity, normed.shape[1]), 'seq',...]
    pallas_call x0 -> x1, Pallas kernels: none -> 108 us  [on_device(): pl.pallas_call(functools.partial(kernel, x_size, z_size), out_shape=jax.S...]
    reduce_scatter x1 -> x0, waiting for transfers between devices: 38.7 us -> none  [on_device(): lax.psum_scatter(partial_value.astype(jnp.float32).astype(jnp.bfloat16),...]
    all_to_all x2 -> x0, starting transfers between devices: 37.6 us -> none  [the longest x1 20.9 us: on_device(): lax.all_to_all(buffer.reshape(experts, capacity, normed.shape[1]), 'seq',...]
    dot_general x2 -> x0, matrix products: 11.9 us -> none  [the longest x1 7.54 us: on_device(): jnp.dot(activated, down_weight[0], preferred_element_type=jnp.float32)]
    scatter x1 -> x0, local copies, waits for them, and re-layouts: 10.2 us -> none  [on_device(): buffer = buffer.at[destination].set(normed[owner_row])]
    reshape x1 -> x0, local copies, waits for them, and re-layouts: 5.31 us -> none  [on_device(): rounded.reshape(received.shape[0], received.shape[1], features)]
    optimization_barrier x1 -> x0, local copies, waits for them, and re-layouts: 4.61 us -> none  [on_device(): rounded = lax.optimization_barrier(partial_value.astype(jnp.bfloat16))]
  transfers between devices with their start and end apart: 3 -> 0, of which waited for: 3 -> 0; matrix products, arithmetic and copies ran while one was open for 0% -> 0% of each run, Pallas kernels for 0% -> 0%
where the time goes in v1:
time: 113 us
  Pallas kernels  108 us (96%)
  local copies, waits for them, and re-layouts  3.53 us (3%)
  other arithmetic  1.55 us (1%)
    pallas_call x1, Pallas kernels, on_device(): pl.pallas_call(functools.partial(kernel, x_size, z_size), out_shape=jax.S...  108 us

profile of v1, /device:TPU:1, one launch (start us, length us, event | category | flops | bytes accessed | tf_op | source)
XLA Modules:
  0.0 113.3 jit_solution(7951425599203550999)
XLA Ops:
  0.0 0.0 copy-start
  0.0 0.0 copy-start.3
  0.0 0.0 copy-start.4
  0.0 0.0 copy-start.5
  0.0 0.0 copy-start.1
  0.0 0.0 copy-start.2
  0.0 1.2 %copy.11 = bf16[128,1440]{1,0:T(8,128)(2,1)S(1)} copy(bf16[128,1440]{0,1:T(8,128)(2,1)} %param.10) | data formatting | bytes 737280 | tf_op args[0]
  1.3 0.2 fusion
  1.4 0.0 copy-done
  1.4 0.2 fusion.2
  1.6 0.7 pad_dynamic-slice_fusion.own_ref
  2.3 0.0 copy-done.3
  2.3 0.0 copy-done.4
  2.3 0.0 copy-done.5
  2.3 0.6 select_maximum_fusion.bias_ref
  2.9 0.0 copy-done.1
  2.9 0.0 copy-done.2
  2.9 0.6 pad_maximum_fusion.meta_ref
  3.5 108.2 %shard_map.100 = bf16[128,360]{1,0:T(8,128)(2,1)} custom-call(bf16[128,384]{1,0:T(8,128)(2,1)} %pad_dynamic-slice_fusion.own_ref, f32[8,128]{1,0:T(8,128)} %pad_maximum_fusion.meta_ref, f32[8,384]{1,0:T(8,128)} %select_maximum_fusion.bias_ref, bf16[1,1440,360]{2,1,0:T(8,128)(2,1)} %wg_hbm.1, bf16[1,1440,360]{2,1,0:T(8,128)(2,1)} %wu_hbm.1, ...), custom_call_target="tpu_custom_call" | custom-call | tf_op jit(solution)/shard_map/pallas_call | solution.py:466
  111.7 1.6 %copy.12 = bf16[128,360]{0,1:T(8,128)(2,1)} copy(bf16[128,360]{1,0:T(8,128)(2,1)} %shard_map.100) | data formatting | bytes 184320 | tf_op jit(solution)/shard_map/pallas_call | solution.py:466
  (2 shorter events, 0.0 us)
Async XLA Ops:
  0.0 1.4 %copy-start = (f32[1440]{0:T(1024)S(1)}, f32[1440]{0:T(1024)}, u32[]{:S(2)}) copy-start(f32[1440]{0:T(1024)} %param.11) | copy-start | bytes 17284
  0.0 2.3 %copy-start.3 = (f32[1,360]{1,0:T(1,128)S(1)}, f32[1,360]{1,0:T(1,128)}, u32[]{:S(2)}) copy-start(f32[1,360]{1,0:T(1,128)} %param.19) | copy-start | bytes 4324
  0.0 2.3 %copy-start.4 = (f32[1,360]{1,0:T(1,128)S(1)}, f32[1,360]{1,0:T(1,128)}, u32[]{:S(2)}) copy-start(f32[1,360]{1,0:T(1,128)} %param.17) | copy-start | bytes 4324
  0.0 2.3 %copy-start.5 = (f32[1,360]{1,0:T(1,128)S(1)}, f32[1,360]{1,0:T(1,128)}, u32[]{:S(2)}) copy-start(f32[1,360]{1,0:T(1,128)} %param.15) | copy-start | bytes 4324
  0.0 2.9 %copy-start.1 = (s32[128,4]{0,1:T(4,128)S(1)}, s32[128,4]{0,1:T(4,128)}, u32[]{:S(2)}) copy-start(s32[128,4]{0,1:T(4,128)} %param.12) | copy-start | bytes 6148
  0.0 2.9 %copy-start.2 = (f32[128,4]{0,1:T(4,128)S(1)}, f32[128,4]{0,1:T(4,128)}, u32[]{:S(2)}) copy-start(f32[128,4]{0,1:T(4,128)} %param.13) | copy-start | bytes 6148

commit v2 on v1

--- a/solution.py
+++ b/solution.py
@@ -15,18 +15,31 @@
 BLOCK = 384
 SLOTS = 8
 PAIR = 2 * SLOTS
+CUTS = 4
 
 
 def kernel(
     x_size,
     z_size,
-    own_ref,
-    meta_ref,
-    bias_ref,
+    tokens_hbm,
+    gain_hbm,
+    ids_hbm,
+    route_hbm,
+    bg_hbm,
+    bu_hbm,
+    bd_hbm,
     wg_hbm,
     wu_hbm,
     wd_hbm,
     out_ref,
+    tokens_s,
+    gain_s,
+    ids_s,
+    route_s,
+    bg_s,
+    bu_s,
+    bd_s,
+    bias_ref,
     tok,
     meta,
     rows_out,
@@ -47,6 +60,7 @@
     acc_s,
     acc_r,
     upper,
+    i_sem,
     w_sem,
     z_send,
     z_recv,
@@ -70,9 +84,10 @@
     stages = half_z
     group = x_size * CORES
     rows = group * PAIR
-    tokens = own_ref.shape[0]
-    half = tokens // 2
-    quarter = out_ref.shape[1]
+    tokens = tok.shape[2]
+    piece = tokens // CUTS
+    side = group // 2
+    quarter = out_ref.shape[0]
     xi = seq // (z_size * CORES)
     zi = (seq // CORES) % z_size
     ci = seq % CORES
@@ -88,6 +103,23 @@
         return (y + 4 + step) % 4
 
     z_up, z_down = at_z(1), at_z(-1)
+
+    small = [
+        pltpu.make_async_copy(src, dst, i_sem.at[i])
+        for i, (src, dst) in enumerate(
+            (
+                (tokens_hbm, tokens_s),
+                (gain_hbm, gain_s),
+                (ids_hbm, ids_s),
+                (route_hbm, route_s),
+                (bg_hbm, bg_s),
+                (bu_hbm, bu_s),
+                (bd_hbm, bd_s),
+            )
+        )
+    ]
+    for copy in small:
+        copy.start()
 
     barrier = pltpu.get_barrier_semaphore()
     for peer in (z_up, z_down):
@@ -106,12 +138,11 @@
     ]
     for copy in weights:
         copy.start()
-    pl.semaphore_wait(barrier, 2 + (group - 1) + 2)
 
     def z_copy(way, k, h, src):
         return pltpu.make_async_remote_copy(
-            src_ref=src.at[pl.ds(h * half, half)],
-            dst_ref=tok.at[k, way, pl.ds(h * half, half)],
+            src_ref=src.at[pl.ds(h * piece, piece)],
+            dst_ref=tok.at[k, way, pl.ds(h * piece, piece)],
             send_sem=z_send.at[way, k, h],
             recv_sem=z_recv.at[way, k, h],
             device_id=(z_up if way else z_down, y),
@@ -128,19 +159,40 @@
             device_id_type=MESH,
         )
 
+    for copy in small:
+        copy.wait()
+    values = tokens_s[...].astype(F32)
+    features = values.shape[0]
+    scale = lax.rsqrt(jnp.sum(values * values, axis=0, keepdims=True) / features + 1e-05)
+    for q in range(4):
+        width = min(BLOCK, features - q * BLOCK)
+
+        @pl.when(y == q)
+        def _():
+            at = slice(q * BLOCK, q * BLOCK + width)
+            normed = (tokens_s[at, :].astype(F32) * scale).T * gain_s[at].reshape(1, width)
+            if width < BLOCK:
+                tok[0, 1] = jnp.zeros((tokens, BLOCK), BF16)
+            tok[0, 1, :, 0:width] = normed.astype(BF16)
+
+    meta[0, 1] = jnp.concatenate([ids_s[...].astype(F32), route_s[...]], axis=0)
+    pl.semaphore_wait(barrier, 2 + (group - 1) + 2)
     for way in (0, 1):
-        m_copy(way, way, meta_ref).start()
-        for h in (0, 1):
-            z_copy(way, way, h, own_ref).start()
-
-    tok[0, 1] = own_ref[...]
-    meta[0, 1] = meta_ref[...]
+        m_copy(way, way, meta.at[0, 1]).start()
+    for h in range(CUTS):
+        for way in (0, 1):
+            z_copy(way, way, h, tok.at[0, 1]).start()
+
+    hidden = bg_s.shape[1]
+    bias_ref[...] = jnp.zeros_like(bias_ref)
+    bias_ref[0:1, 0:hidden] = bg_s[...]
+    bias_ref[1:2, 0:hidden] = bu_s[...]
+    bias_ref[2:3, 0:quarter] = bd_s[...]
     upper[...] = (
         lax.broadcasted_iota(jnp.int32, (tokens, tokens), 0)
         < lax.broadcasted_iota(jnp.int32, (tokens, tokens), 1)
     ).astype(BF16)
 
-    features, hidden = wg_s.shape
     w_in[...] = jnp.zeros_like(w_in)
     w_out[...] = jnp.zeros_like(w_out)
     for copy in weights:
@@ -189,39 +241,36 @@
     def b_local(k):
         return pltpu.make_async_copy(out_rows.at[k, me], back.at[k, me], b_loc.at[k])
 
-    def sign(k):
-        return 1 - 2 * (k % 2)
-
-    def y_copy(k, kind):
-        s = sign(k)
+    def y_copy(k, kind, h):
+        s = 1 - 2 * h
         block = at_y(-s) if kind == 2 else y
-        to = at_y(-s) if kind == 1 else at_y(s)
-        return pltpu.make_async_remote_copy(
-            src_ref=in_rows.at[k, block],
-            dst_ref=in_rows.at[k, block],
-            send_sem=y_send.at[kind, k],
-            recv_sem=y_recv.at[kind, k],
-            device_id=(seq, to),
-            device_id_type=MESH,
-        )
-
-    def r_copy(k, kind):
-        s = sign(k)
-        to = at_y(-s) if kind == 1 else at_y(s)
-        src = rs_t.at[k] if kind == 2 else part.at[k, at_y(2) if kind == 0 else at_y(-s)]
+        at = in_rows.at[k, block, pl.ds(h * side, side)]
+        return pltpu.make_async_remote_copy(
+            src_ref=at,
+            dst_ref=at,
+            send_sem=y_send.at[kind, k, h],
+            recv_sem=y_recv.at[kind, k, h],
+            device_id=(seq, at_y(-s) if kind == 1 else at_y(s)),
+            device_id_type=MESH,
+        )
+
+    def r_copy(k, kind, h):
+        s = 1 - 2 * h
+        at = pl.ds(h * (rows // 2), rows // 2)
+        src = rs_t.at[k, at] if kind == 2 else part.at[k, at_y(2) if kind == 0 else at_y(-s), at]
         return pltpu.make_async_remote_copy(
             src_ref=src,
-            dst_ref=(rs_r, rs_b, rs_a)[kind].at[k],
-            send_sem=r_send.at[kind, k],
-            recv_sem=r_recv.at[kind, k],
-            device_id=(seq, to),
+            dst_ref=(rs_r, rs_b, rs_a)[kind].at[k, at],
+            send_sem=r_send.at[kind, k, h],
+            recv_sem=r_recv.at[kind, k, h],
+            device_id=(seq, at_y(-s) if kind == 1 else at_y(s)),
             device_id_type=MESH,
         )
 
     def c_copy(way, k, h, to_slot):
         return pltpu.make_async_remote_copy(
-            src_ref=acc_s.at[way, k, pl.ds(h * half, half)],
-            dst_ref=acc_r.at[way, to_slot, pl.ds(h * half, half)],
+            src_ref=acc_s.at[way, k, pl.ds(h * piece, piece)],
+            dst_ref=acc_r.at[way, to_slot, pl.ds(h * piece, piece)],
             send_sem=c_send.at[way, k, h],
             recv_sem=c_recv.at[way, to_slot, h],
             device_id=(z_down if way else z_up, y),
@@ -229,33 +278,29 @@
         )
 
     def z_stage(k):
-        @pl.when(k >= 1)
-        def _():
-            m_copy(1, k, meta.at[k, 1]).wait_recv()
-
-            @pl.when(k < stages - 1)
-            def _():
-                m_copy(1, k + 1, meta.at[k, 1]).start()
-
-            for h in (0, 1):
-                z_copy(1, k, h, tok.at[k, 1]).wait_recv()
-
-                @pl.when(k < stages - 1)
-                def _():
-                    z_copy(1, k + 1, h, tok.at[k, 1]).start()
-
-        m_copy(0, k, meta.at[k, 0]).wait_recv()
-
-        @pl.when(k < stages - 1)
-        def _():
-            m_copy(0, k + 1, meta.at[k, 0]).start()
-
-        for h in (0, 1):
-            z_copy(0, k, h, tok.at[k, 0]).wait_recv()
-
-            @pl.when(k < stages - 1)
-            def _():
-                z_copy(0, k + 1, h, tok.at[k, 0]).start()
+        def step(way, wait, forward):
+            def go():
+                wait()
+                pl.when(k < stages - 1)(forward)
+
+            if way:
+                pl.when(k >= 1)(go)
+            else:
+                go()
+
+        for way in (1, 0):
+            step(
+                way,
+                lambda: m_copy(way, k, meta.at[k, way]).wait_recv(),
+                lambda: m_copy(way, k + 1, meta.at[k, way]).start(),
+            )
+        for h in range(CUTS):
+            for way in (1, 0):
+                step(
+                    way,
+                    lambda: z_copy(way, k, h, tok.at[k, way]).wait_recv(),
+                    lambda: z_copy(way, k + 1, h, tok.at[k, way]).start(),
+                )
 
     def dispatch(k):
         picks, mixes = [], []
@@ -294,16 +339,19 @@
         x_local(k).wait()
         whole = in_rows.at[k, y, pl.ds(0, group - 1)]
         pltpu.make_async_copy(whole, whole, x_recv.at[k]).wait()
-        y_copy(k, 0).start()
-        y_copy(k, 1).start()
+        for kind in (0, 1):
+            for h in (0, 1):
+                y_copy(k, kind, h).start()
 
     def y_relay(k):
-        y_copy(k, 0).wait_recv()
-        y_copy(k, 2).start()
+        for h in (0, 1):
+            y_copy(k, 0, h).wait_recv()
+            y_copy(k, 2, h).start()
 
     def compute(k):
-        y_copy(k, 1).wait_recv()
-        y_copy(k, 2).wait_recv()
+        for kind in (1, 2):
+            for h in (0, 1):
+                y_copy(k, kind, h).wait_recv()
         x = jnp.concatenate([in_rows[k, q].reshape(rows, BLOCK) for q in range(4)], axis=1)
         pre = jnp.dot(x, w_in[...], preferred_element_type=F32)
         gate = pre[:, :BLOCK] + bias_ref[0:1, :]
@@ -313,38 +361,33 @@
         for p in range(4):
             part[k, p] = result[:, p * BLOCK : (p + 1) * BLOCK]
 
-    @pl.loop(0, stages + 3)
+    def stage(t, first, go):
+        pl.when((t >= first) & (t < stages + first))(lambda: go(t - first))
+
+    @pl.loop(0, stages + 4)
     def _(t):
-        @pl.when(t < stages)
-        def _():
-            z_stage(t)
-            dispatch(t)
-
-        @pl.when((t >= 1) & (t < stages + 1))
-        def _():
-            y_start(t - 1)
-
-        @pl.when((t >= 2) & (t < stages + 2))
-        def _():
-            y_relay(t - 2)
-
-        @pl.when(t >= 3)
-        def _():
-            compute(t - 3)
-
-    def r_start(k):
-        r_copy(k, 0).start()
-        r_copy(k, 1).start()
+        stage(t, 0, z_stage)
+        stage(t, 0, dispatch)
+        stage(t, 1, y_start)
+        stage(t, 4, compute)
+        stage(t, 2, y_relay)
+
+    def r_start(k, kind):
+        for h in (0, 1):
+            r_copy(k, kind, h).start()
 
     def r_relay(k):
-        r_copy(k, 0).wait_recv()
-        total = rs_r[k].astype(F32) + part[k, at_y(sign(k))].astype(F32)
-        rs_t[k] = total.astype(BF16)
-        r_copy(k, 2).start()
+        for h in (0, 1):
+            at = pl.ds(h * (rows // 2), rows // 2)
+            r_copy(k, 0, h).wait_recv()
+            total = rs_r[k, at].astype(F32) + part[k, at_y(1 - 2 * h), at].astype(F32)
+            rs_t[k, at] = total.astype(BF16)
+            r_copy(k, 2, h).start()
 
     def finish(k):
-        r_copy(k, 1).wait_recv()
-        r_copy(k, 2).wait_recv()
+        for kind in (1, 2):
+            for h in (0, 1):
+                r_copy(k, kind, h).wait_recv()
         total = part[k, y].astype(F32) + rs_b[k].astype(F32) + rs_a[k].astype(F32)
         total = total + bias_ref[2:3, :]
         out_rows[k] = total.astype(BF16).reshape(group, PAIR, BLOCK)
@@ -359,10 +402,11 @@
         came = back[k].reshape(rows, BLOCK)
         came = jnp.concatenate([came, came], axis=0)
         both = jnp.dot(mix[k], came, preferred_element_type=F32)
-        for h in (0, 1):
-            at = pl.ds(h * half, half)
+        for h in range(CUTS):
+            at = pl.ds(h * piece, piece)
             for way in (0, 1):
-                value = both[way * tokens + h * half : way * tokens + (h + 1) * half]
+                first = way * tokens + h * piece
+                value = both[first : first + piece]
 
                 @pl.when(k == stages - 1)
                 def _():
@@ -384,30 +428,21 @@
 
         @pl.when(k == 0)
         def _():
-            for h in (0, 1):
-                at = pl.ds(h * half, half)
-                value = both[tokens + h * half : tokens + (h + 1) * half]
+            for h in range(CUTS):
                 c_copy(0, 0, h, stages - 1).wait_recv()
-                total = value + acc_r[1, 0, at].astype(F32) + acc_r[0, stages - 1, at].astype(F32)
-                out_ref[at, :] = total[:, :quarter].astype(out_ref.dtype)
-
-    @pl.loop(0, stages + 3)
+            total = both[tokens:] + acc_r[1, 0].astype(F32) + acc_r[0, stages - 1].astype(F32)
+            out_ref[...] = total.T[:quarter].astype(out_ref.dtype)
+
+    def turn(go):
+        return lambda n: go(stages - 1 - n)
+
+    @pl.loop(0, stages + 4)
     def _(t):
-        @pl.when(t < stages)
-        def _():
-            r_start(stages - 1 - t)
-
-        @pl.when((t >= 1) & (t < stages + 1))
-        def _():
-            r_relay(stages - t)
-
-        @pl.when((t >= 2) & (t < stages + 2))
-        def _():
-            finish(stages + 1 - t)
-
-        @pl.when(t >= 3)
-        def _():
-            combine(stages + 2 - t)
+        stage(t, 0, turn(lambda k: r_start(k, 0)))
+        stage(t, 3, turn(finish))
+        stage(t, 1, turn(lambda k: r_start(k, 1)))
+        stage(t, 1, turn(r_relay))
+        stage(t, 4, turn(combine))
 
     @pl.loop(0, stages)
     def _(k):
@@ -415,14 +450,15 @@
 
             @pl.when(k >= way)
             def _():
-                m_copy(way, k, meta_ref).wait_send()
-                for h in (0, 1):
-                    z_copy(way, k, h, own_ref).wait_send()
+                m_copy(way, k, meta.at[k, way]).wait_send()
+                for h in range(CUTS):
+                    z_copy(way, k, h, tok.at[k, way]).wait_send()
                     c_copy(way, k, h, k).wait_send()
 
         for kind in range(3):
-            y_copy(k, kind).wait_send()
-            r_copy(k, kind).wait_send()
+            for h in (0, 1):
+                y_copy(k, kind, h).wait_send()
+                r_copy(k, kind, h).wait_send()
         sent = rows_out.at[k, pl.ds(0, group - 1)]
         pltpu.make_async_copy(sent, sent, x_send.at[k]).wait()
         sent = out_rows.at[k, pl.ds(0, group - 1)]
@@ -444,31 +480,29 @@
     tok_rows, features = tokens.shape
     z_size = Z_RING
     x_size = lax.axis_size("seq") // (z_size * CORES)
-    hidden = gate_weight.shape[2]
     quarter = features // 4
     stages = z_size // 2
     group = x_size * CORES
     rows = group * PAIR
-    values = tokens.astype(F32)
-    normed = (
-        values * lax.rsqrt(jnp.mean(values * values, axis=-1, keepdims=True) + 1e-05) * norm_gain
-    ).astype(BF16)
-    normed = jnp.pad(normed, ((0, 0), (0, 4 * BLOCK - features)))
-    own = lax.dynamic_slice(normed, (0, lax.axis_index("rep") * BLOCK), (tok_rows, BLOCK))
-    meta = jnp.concatenate([expert_ids.T.astype(F32), route_weights.T], axis=0)
-    bias = jnp.concatenate([gate_bias, up_bias, down_bias], axis=0)
-    bias = jnp.pad(bias, ((0, 5), (0, BLOCK - hidden)))
 
     block = (stages, rows, BLOCK)
     vmem = pl.BlockSpec(memory_space=pltpu.VMEM)
     hbm = pl.BlockSpec(memory_space=pl.ANY)
     dma = pltpu.SemaphoreType.DMA
-    return pl.pallas_call(
+    mixed = pl.pallas_call(
         functools.partial(kernel, x_size, z_size),
-        out_shape=jax.ShapeDtypeStruct((tok_rows, quarter), BF16),
-        in_specs=[vmem, vmem, vmem, hbm, hbm, hbm],
+        out_shape=pltpu.VMEM((quarter, tok_rows), BF16),
+        in_specs=[hbm] * 10,
         out_specs=vmem,
         scratch_shapes=[
+            pltpu.VMEM((features, tok_rows), BF16),
+            pltpu.VMEM((features,), F32),
+            pltpu.VMEM((4, tok_rows), jnp.int32),
+            pltpu.VMEM((4, tok_rows), F32),
+            pltpu.VMEM(gate_bias.shape, F32),
+            pltpu.VMEM(up_bias.shape, F32),
+            pltpu.VMEM(down_bias.shape, F32),
+            pltpu.VMEM((8, BLOCK), F32),
             pltpu.VMEM((stages, 2, tok_rows, BLOCK), BF16),
             pltpu.VMEM((stages, 2, 8, tok_rows), F32),
             pltpu.VMEM((stages, group, PAIR, BLOCK), BF16),
@@ -489,28 +523,41 @@
             pltpu.VMEM((2, stages, tok_rows, BLOCK), BF16),
             pltpu.VMEM((2, stages, tok_rows, BLOCK), BF16),
             pltpu.VMEM((tok_rows, tok_rows), BF16),
+            dma((7,)),
             dma((3,)),
-            dma((2, stages, 2)),
-            dma((2, stages, 2)),
+            dma((2, stages, CUTS)),
+            dma((2, stages, CUTS)),
             dma((2, stages)),
             dma((2, stages)),
             dma((stages,)),
             dma((stages,)),
             dma((stages,)),
-            dma((3, stages)),
-            dma((3, stages)),
-            dma((3, stages)),
-            dma((3, stages)),
+            dma((3, stages, 2)),
+            dma((3, stages, 2)),
+            dma((3, stages, 2)),
+            dma((3, stages, 2)),
             dma((stages,)),
             dma((stages,)),
             dma((stages,)),
-            dma((2, stages, 2)),
-            dma((2, stages, 2)),
+            dma((2, stages, CUTS)),
+            dma((2, stages, CUTS)),
         ],
         compiler_params=pltpu.CompilerParams(
             collective_id=0, has_side_effects=True, vmem_limit_bytes=56 * 1024 * 1024
         ),
-    )(own, meta, bias, gate_weight, up_weight, down_weight)
+    )(
+        tokens.T,
+        norm_gain,
+        expert_ids.T,
+        route_weights.T,
+        gate_bias,
+        up_bias,
+        down_bias,
+        gate_weight,
+        up_weight,
+        down_weight,
+    )
+    return mixed.T
 
 
 def solution(mesh):

time: 113 us -> 99.5 us (0.88)
  Pallas kernels: 108 us -> 98.7 us
  local copies, waits for them, and re-layouts: 3.53 us -> 0.64 us
  other arithmetic: 1.55 us -> 0 us
    pallas_call x1, Pallas kernels: 108 us -> 98.7 us  [on_device(): pl.pallas_call(functools.partial(kernel, x_size, z_size), out_shape=pltpu...]
    pallas_call x1 -> x0, local copies, waits for them, and re-layouts: 1.64 us -> none  [on_device(): pl.pallas_call(functools.partial(kernel, x_size, z_size), out_shape=jax.S...]
    concatenate x2 -> x0, other arithmetic: 1.21 us -> none  [the longest x1 0.61 us: on_device(): bias = jnp.concatenate([gate_bias, up_bias, down_bias], axis=0)]
where the time goes in v2:
time: 99.5 us; the launch traced here: 99.4 us
  Pallas kernels  98.7 us (99%)
    pallas_call x1, Pallas kernels, on_device(): pl.pallas_call(functools.partial(kernel, x_size, z_size), out_shape=pltpu...  98.7 us

profile of v2, /device:TPU:1, one launch (start us, length us, event | category | flops | bytes accessed | tf_op | source)
XLA Modules:
  0.0 99.4 jit_solution(13184798888337036375)
XLA Ops:
  0.0 98.7 %shard_map.100 = bf16[360,128]{1,0:T(8,128)(2,1)S(1)} custom-call(bf16[1440,128]{1,0:T(8,128)(2,1)} %bitcast.5, f32[1440]{0:T(1024)} %gain_hbm.1, s32[4,128]{1,0:T(4,128)} %bitcast.6, f32[4,128]{1,0:T(4,128)} %bitcast.7, f32[1,360]{1,0:T(1,128)} %bg_hbm.1, f32[1,360]{1,0:T(1,128)} %bu_hbm.1, f32[1,360]{1,0:T(1,128)} %bd_hbm.1, bf16[1,1440,360]{2,1,0:T(8,128)(2,1)} %wg_hbm.1, ...), custom_call_target="tpu_custom_call" | custom-call | tf_op jit(solution)/shard_map/pallas_call | solution.py:492
  98.7 0.6 copy.12

commit v3 on v2

--- a/solution.py
+++ b/solution.py
@@ -51,8 +51,7 @@
     wd_s,
     part,
     rs_r,
-    rs_a,
-    rs_b,
+    rs_n,
     rs_t,
     out_rows,
     back,
@@ -71,8 +70,10 @@
     x_loc,
     y_send,
     y_recv,
+    y_near,
     r_send,
     r_recv,
+    r_near,
     b_send,
     b_recv,
     b_loc,
@@ -139,11 +140,14 @@
     for copy in weights:
         copy.start()
 
+    def arrived(ref, sem):
+        pltpu.make_async_copy(ref, ref, sem).wait()
+
     def z_copy(way, k, h, src):
         return pltpu.make_async_remote_copy(
             src_ref=src.at[pl.ds(h * piece, piece)],
             dst_ref=tok.at[k, way, pl.ds(h * piece, piece)],
-            send_sem=z_send.at[way, k, h],
+            send_sem=z_send.at[way],
             recv_sem=z_recv.at[way, k, h],
             device_id=(z_up if way else z_down, y),
             device_id_type=MESH,
@@ -153,7 +157,7 @@
         return pltpu.make_async_remote_copy(
             src_ref=src,
             dst_ref=meta.at[k, way],
-            send_sem=m_send.at[way, k],
+            send_sem=m_send.at[way],
             recv_sem=m_recv.at[way, k],
             device_id=(z_up if way else z_down, y),
             device_id_type=MESH,
@@ -177,11 +181,11 @@
 
     meta[0, 1] = jnp.concatenate([ids_s[...].astype(F32), route_s[...]], axis=0)
     pl.semaphore_wait(barrier, 2 + (group - 1) + 2)
-    for way in (0, 1):
-        m_copy(way, way, meta.at[0, 1]).start()
     for h in range(CUTS):
         for way in (0, 1):
             z_copy(way, way, h, tok.at[0, 1]).start()
+    for way in (0, 1):
+        m_copy(way, way, meta.at[0, 1]).start()
 
     hidden = bg_s.shape[1]
     bias_ref[...] = jnp.zeros_like(bias_ref)
@@ -218,7 +222,7 @@
         return pltpu.make_async_remote_copy(
             src_ref=rows_out.at[k, e],
             dst_ref=in_rows.at[k, y, me],
-            send_sem=x_send.at[k],
+            send_sem=x_send.at[0],
             recv_sem=x_recv.at[k],
             device_id=(at_x(e), y),
             device_id_type=MESH,
@@ -232,7 +236,7 @@
         return pltpu.make_async_remote_copy(
             src_ref=out_rows.at[k, e],
             dst_ref=back.at[k, me],
-            send_sem=b_send.at[k],
+            send_sem=b_send.at[0],
             recv_sem=b_recv.at[k],
             device_id=(at_x(e), y),
             device_id_type=MESH,
@@ -248,8 +252,8 @@
         return pltpu.make_async_remote_copy(
             src_ref=at,
             dst_ref=at,
-            send_sem=y_send.at[kind, k, h],
-            recv_sem=y_recv.at[kind, k, h],
+            send_sem=y_send.at[kind],
+            recv_sem=y_recv.at[k, h] if kind == 0 else y_near.at[k],
             device_id=(seq, at_y(-s) if kind == 1 else at_y(s)),
             device_id_type=MESH,
         )
@@ -260,9 +264,9 @@
         src = rs_t.at[k, at] if kind == 2 else part.at[k, at_y(2) if kind == 0 else at_y(-s), at]
         return pltpu.make_async_remote_copy(
             src_ref=src,
-            dst_ref=(rs_r, rs_b, rs_a)[kind].at[k, at],
-            send_sem=r_send.at[kind, k, h],
-            recv_sem=r_recv.at[kind, k, h],
+            dst_ref=rs_n.at[k, kind - 1, at] if kind else rs_r.at[k, at],
+            send_sem=r_send.at[kind],
+            recv_sem=r_recv.at[k, h] if kind == 0 else r_near.at[k],
             device_id=(seq, at_y(-s) if kind == 1 else at_y(s)),
             device_id_type=MESH,
         )
@@ -271,7 +275,7 @@
         return pltpu.make_async_remote_copy(
             src_ref=acc_s.at[way, k, pl.ds(h * piece, piece)],
             dst_ref=acc_r.at[way, to_slot, pl.ds(h * piece, piece)],
-            send_sem=c_send.at[way, k, h],
+            send_sem=c_send.at[way],
             recv_sem=c_recv.at[way, to_slot, h],
             device_id=(z_down if way else z_up, y),
             device_id_type=MESH,
@@ -288,12 +292,6 @@
             else:
                 go()
 
-        for way in (1, 0):
-            step(
-                way,
-                lambda: m_copy(way, k, meta.at[k, way]).wait_recv(),
-                lambda: m_copy(way, k + 1, meta.at[k, way]).start(),
-            )
         for h in range(CUTS):
             for way in (1, 0):
                 step(
@@ -301,6 +299,12 @@
                     lambda: z_copy(way, k, h, tok.at[k, way]).wait_recv(),
                     lambda: z_copy(way, k + 1, h, tok.at[k, way]).start(),
                 )
+        for way in (1, 0):
+            step(
+                way,
+                lambda: m_copy(way, k, meta.at[k, way]).wait_recv(),
+                lambda: m_copy(way, k + 1, meta.at[k, way]).start(),
+            )
 
     def dispatch(k):
         picks, mixes = [], []
@@ -337,8 +341,7 @@
 
     def y_start(k):
         x_local(k).wait()
-        whole = in_rows.at[k, y, pl.ds(0, group - 1)]
-        pltpu.make_async_copy(whole, whole, x_recv.at[k]).wait()
+        arrived(in_rows.at[k, y, pl.ds(0, group - 1)], x_recv.at[k])
         for kind in (0, 1):
             for h in (0, 1):
                 y_copy(k, kind, h).start()
@@ -349,9 +352,7 @@
             y_copy(k, 2, h).start()
 
     def compute(k):
-        for kind in (1, 2):
-            for h in (0, 1):
-                y_copy(k, kind, h).wait_recv()
+        arrived(in_rows.at[k, pl.ds(0, 2)], y_near.at[k])
         x = jnp.concatenate([in_rows[k, q].reshape(rows, BLOCK) for q in range(4)], axis=1)
         pre = jnp.dot(x, w_in[...], preferred_element_type=F32)
         gate = pre[:, :BLOCK] + bias_ref[0:1, :]
@@ -364,13 +365,13 @@
     def stage(t, first, go):
         pl.when((t >= first) & (t < stages + first))(lambda: go(t - first))
 
-    @pl.loop(0, stages + 4)
+    @pl.loop(0, stages + 5)
     def _(t):
         stage(t, 0, z_stage)
+        stage(t, 3, y_relay)
         stage(t, 0, dispatch)
         stage(t, 1, y_start)
-        stage(t, 4, compute)
-        stage(t, 2, y_relay)
+        stage(t, 5, compute)
 
     def r_start(k, kind):
         for h in (0, 1):
@@ -385,10 +386,8 @@
             r_copy(k, 2, h).start()
 
     def finish(k):
-        for kind in (1, 2):
-            for h in (0, 1):
-                r_copy(k, kind, h).wait_recv()
-        total = part[k, y].astype(F32) + rs_b[k].astype(F32) + rs_a[k].astype(F32)
+        arrived(rs_n.at[k], r_near.at[k])
+        total = part[k, y].astype(F32) + rs_n[k, 0].astype(F32) + rs_n[k, 1].astype(F32)
         total = total + bias_ref[2:3, :]
         out_rows[k] = total.astype(BF16).reshape(group, PAIR, BLOCK)
         b_local(k).start()
@@ -397,8 +396,7 @@
 
     def combine(k):
         b_local(k).wait()
-        whole = back.at[k, pl.ds(0, group - 1)]
-        pltpu.make_async_copy(whole, whole, b_recv.at[k]).wait()
+        arrived(back.at[k, pl.ds(0, group - 1)], b_recv.at[k])
         came = back[k].reshape(rows, BLOCK)
         came = jnp.concatenate([came, came], axis=0)
         both = jnp.dot(mix[k], came, preferred_element_type=F32)
@@ -444,25 +442,16 @@
         stage(t, 1, turn(r_relay))
         stage(t, 4, turn(combine))
 
-    @pl.loop(0, stages)
-    def _(k):
-        for way in (0, 1):
-
-            @pl.when(k >= way)
-            def _():
-                m_copy(way, k, meta.at[k, way]).wait_send()
-                for h in range(CUTS):
-                    z_copy(way, k, h, tok.at[k, way]).wait_send()
-                    c_copy(way, k, h, k).wait_send()
-
-        for kind in range(3):
-            for h in (0, 1):
-                y_copy(k, kind, h).wait_send()
-                r_copy(k, kind, h).wait_send()
-        sent = rows_out.at[k, pl.ds(0, group - 1)]
-        pltpu.make_async_copy(sent, sent, x_send.at[k]).wait()
-        sent = out_rows.at[k, pl.ds(0, group - 1)]
-        pltpu.make_async_copy(sent, sent, b_send.at[k]).wait()
+    for way in (0, 1):
+        sent = pl.ds(0, stages - way)
+        arrived(meta.at[sent, way], m_send.at[way])
+        arrived(tok.at[sent, way], z_send.at[way])
+        arrived(acc_s.at[way, sent], c_send.at[way])
+    for kind in range(3):
+        arrived(in_rows.at[:, y], y_send.at[kind])
+        arrived(rs_r, r_send.at[kind])
+    arrived(rows_out.at[:, pl.ds(0, group - 1)], x_send.at[0])
+    arrived(out_rows.at[:, pl.ds(0, group - 1)], b_send.at[0])
 
 
 def on_device(
@@ -514,8 +503,7 @@
             pltpu.VMEM(down_weight.shape[1:], BF16),
             pltpu.VMEM((stages, 4, rows, BLOCK), BF16),
             pltpu.VMEM(block, BF16),
-            pltpu.VMEM(block, BF16),
-            pltpu.VMEM(block, BF16),
+            pltpu.VMEM((stages, 2, rows, BLOCK), BF16),
             pltpu.VMEM(block, BF16),
             pltpu.VMEM((stages, group, PAIR, BLOCK), BF16),
             pltpu.VMEM((stages, group, PAIR, BLOCK), BF16),
@@ -525,21 +513,23 @@
             pltpu.VMEM((tok_rows, tok_rows), BF16),
             dma((7,)),
             dma((3,)),
+            dma((2,)),
             dma((2, stages, CUTS)),
-            dma((2, stages, CUTS)),
+            dma((2,)),
             dma((2, stages)),
-            dma((2, stages)),
+            dma((1,)),
             dma((stages,)),
             dma((stages,)),
+            dma((3,)),
+            dma((stages, 2)),
             dma((stages,)),
-            dma((3, stages, 2)),
-            dma((3, stages, 2)),
-            dma((3, stages, 2)),
-            dma((3, stages, 2)),
+            dma((3,)),
+            dma((stages, 2)),
+            dma((stages,)),
+            dma((1,)),
             dma((stages,)),
             dma((stages,)),
-            dma((stages,)),
-            dma((2, stages, CUTS)),
+            dma((2,)),
             dma((2, stages, CUTS)),
         ],
         compiler_params=pltpu.CompilerParams(

time: 99.5 us -> 96 us (0.965); the launches traced: 99.4 us -> 94.8 us
  Pallas kernels: 98.7 us -> 94.1 us
    pallas_call x1, Pallas kernels: 98.7 us -> 94.1 us  [on_device(): pl.pallas_call(functools.partial(kernel, x_size, z_size), out_shape=pltpu...]
where the time goes in v3:
time: 96 us; the launch traced here: 94.8 us
  Pallas kernels  94.1 us (98%)
    pallas_call x1, Pallas kernels, on_device(): pl.pallas_call(functools.partial(kernel, x_size, z_size), out_shape=pltpu...  94.1 us

profile of v3, /device:TPU:1, one launch (start us, length us, event | category | flops | bytes accessed | tf_op | source)
XLA Modules:
  0.0 94.8 jit_solution(18100332434141879514)
XLA Ops:
  0.0 94.1 %shard_map.100 = bf16[360,128]{1,0:T(8,128)(2,1)S(1)} custom-call(bf16[1440,128]{1,0:T(8,128)(2,1)} %bitcast.5, f32[1440]{0:T(1024)} %gain_hbm.1, s32[4,128]{1,0:T(4,128)} %bitcast.6, f32[4,128]{1,0:T(4,128)} %bitcast.7, f32[1,360]{1,0:T(1,128)} %bg_hbm.1, f32[1,360]{1,0:T(1,128)} %bu_hbm.1, f32[1,360]{1,0:T(1,128)} %bd_hbm.1, bf16[1,1440,360]{2,1,0:T(8,128)(2,1)} %wg_hbm.1, ...), custom_call_target="tpu_custom_call" | custom-call | tf_op jit(solution)/shard_map/pallas_call | solution.py:481
  94.1 0.6 copy.12
